TPU v7x, 32 devices: a whole 2x2x4 slice. The times are simulated.
32 devices in a mesh: scan: 2 (over x), tile: 16 (over z, y, core).
Axes of the slice: x: 2, y: 2, z: 4, core: 2. Of those that a mesh axis runs over, the one named last changes fastest.
Arguments:
- slices: float32 [4, 2, 1024, 1024], P(None, None, ('scan', 'tile')), parts along dimension 2, may hold values from -4 to 4
- probe_modes: float32 [4, 2, 128, 128], P('scan'), parts along dimension 0, may hold values from -4 to 4
- row_offset: int32 [128], P(('scan', 'tile')), parts along dimension 0, may hold values from 0 to 31, as said below
- col_offset: int32 [128], P(('scan', 'tile')), parts along dimension 0, may hold values from 0 to 1023
- amplitude: float32 [128, 128, 128], P(('scan', 'tile')), parts along dimension 0, may hold values from 0.5 to 3
Outputs:
- slice_grad: float32 [4, 2, 1024, 1024], P(None, None, ('scan', 'tile')), parts along dimension 2
- probe_grad: float32 [4, 2, 128, 128], P('scan'), parts along dimension 0
There are 2 independent parts, one for each index of `scan`. A program takes and returns all parts, laid end to end along the dimension named above; each array names one. Nothing has to cross between parts.
Inputs may be any that keep to these rules, and one draw needn't show every extreme that they name: Window w starts 32 * (w // 4) + row_offset[w] rows down the object; the largest value is taken by some window in every draw.
All inputs are finite; a program needn't handle non-finite values.
Results may differ from a plain program's by a relative error of at most 0.0003.
Values sent between devices are 32-bit elements; how exact they have to be, the bound alone decides.
A program may use at most 128 MiB of HBM per device.

v0:
```python
import math

import jax
import jax.numpy as jnp
from jax import lax
from jax.sharding import PartitionSpec as P

INTENSITY_SHIFT = 0.5
FRESNEL = 0.75


def from_behind(value, axis, steps):
    count = lax.axis_size(axis)
    pairs = [(source, (source + steps) % count) for source in range(count)]
    return lax.ppermute(value, axis, pairs)


def dft_tables(window_side):
    steps_idx = jnp.arange(window_side, dtype=jnp.int32)
    product = steps_idx[:, None] * steps_idx[None, :] % window_side
    angles = product.astype(jnp.float32) * (-2.0 * math.pi / window_side)
    scale = 1.0 / math.sqrt(window_side)
    return (jnp.cos(angles) * scale, jnp.sin(angles) * scale)


def fresnel_kernel(window_side):
    steps_idx = jnp.arange(window_side, dtype=jnp.int32)
    freqs = (steps_idx + window_side // 2) % window_side - window_side // 2
    radius = (freqs[:, None] * freqs[:, None] + freqs[None, :] * freqs[None, :]).astype(jnp.float32)
    phase = radius * (-math.pi * FRESNEL / (window_side / 2.0) ** 2)
    return (jnp.cos(phase), jnp.sin(phase))


def left_apply(mat_real, mat_imag, wave_real, wave_imag):

    def product(matrix, field):
        return jnp.einsum("jk,mkl->mjl", matrix, field, precision=lax.Precision.HIGHEST)

    return (
        product(mat_real, wave_real) - product(mat_imag, wave_imag),
        product(mat_real, wave_imag) + product(mat_imag, wave_real),
    )


def right_apply(wave_real, wave_imag, mat_real, mat_imag):

    def product(field, matrix):
        return jnp.einsum("mjk,kl->mjl", field, matrix, precision=lax.Precision.HIGHEST)

    return (
        product(wave_real, mat_real) - product(wave_imag, mat_imag),
        product(wave_imag, mat_real) + product(wave_real, mat_imag),
    )


def transform(wave_real, wave_imag, mat_real, mat_imag):
    half_real, half_imag = left_apply(mat_real, mat_imag, wave_real, wave_imag)
    return right_apply(half_real, half_imag, mat_real, mat_imag)


def propagate(wave_real, wave_imag, tables):
    cos_table, sin_table, kernel_real, kernel_imag = tables
    spec_real, spec_imag = transform(wave_real, wave_imag, cos_table, sin_table)
    moved_real = spec_real * kernel_real - spec_imag * kernel_imag
    moved_imag = spec_real * kernel_imag + spec_imag * kernel_real
    return transform(moved_real, moved_imag, cos_table, -sin_table)


def window_loss(crops, probe_modes, measured, tables):
    cos_table, sin_table = (tables[0], tables[1])
    wave_real = probe_modes[:, 0]
    wave_imag = probe_modes[:, 1]
    slice_count = crops.shape[0]
    exit_real = wave_real
    exit_imag = wave_imag
    for depth_index in range(slice_count):
        trans_real = crops[depth_index, 0]
        trans_imag = crops[depth_index, 1]
        exit_real = trans_real * wave_real - trans_imag * wave_imag
        exit_imag = trans_real * wave_imag + trans_imag * wave_real
        if depth_index + 1 < slice_count:
            wave_real, wave_imag = propagate(exit_real, exit_imag, tables)
    far_real, far_imag = transform(exit_real, exit_imag, cos_table, sin_table)
    intensity = jnp.sum(far_real * far_real + far_imag * far_imag, axis=0)
    modelled = jnp.sqrt(intensity + INTENSITY_SHIFT)
    return 0.5 * jnp.sum((modelled - measured) ** 2)


def window_grads(crops, probe_modes, measured, tables):
    return jax.grad(window_loss, argnums=(0, 1))(crops, probe_modes, measured, tables)


def on_device(slices, probe_modes, row_offset, col_offset, amplitude):
    window_side = probe_modes.shape[-1]
    slice_count = slices.shape[0]
    rows_here = slices.shape[2]
    cols_here = slices.shape[3]
    upper_count = (window_side - 2) // rows_here + 1
    cos_table, sin_table = dft_tables(window_side)
    kernel_real, kernel_imag = fresnel_kernel(window_side)
    tables = (cos_table, sin_table, kernel_real, kernel_imag)
    pieces = [slices]
    moving = slices
    for offset in range(upper_count):
        moving = from_behind(moving, "tile", -1)
        pieces.append(moving)
    extended = jnp.concatenate(pieces, axis=2)[:, :, : rows_here + window_side - 1]
    extended = jnp.concatenate([extended, extended[:, :, :, : window_side - 1]], axis=3)
    anchor = jnp.zeros((), jnp.int32)
    crop_shape = (slice_count, 2, window_side, window_side)

    def one_window(row_start, col_start, measured):
        corner = (anchor, anchor, row_start, col_start)
        crops = lax.dynamic_slice(extended, corner, crop_shape)
        return window_grads(crops, probe_modes, measured, tables)

    crop_grads, probe_terms = jax.vmap(one_window)(row_offset, col_offset, amplitude)

    def add_window(window_index, gradient_buffer):
        corner = (anchor, anchor, row_offset[window_index], col_offset[window_index])
        current = lax.dynamic_slice(gradient_buffer, corner, crop_shape)
        return lax.dynamic_update_slice(gradient_buffer, current + crop_grads[window_index], corner)

    gradient_buffer = lax.fori_loop(
        0, row_offset.shape[0], add_window, jnp.zeros(extended.shape, jnp.float32)
    )
    folded = (
        gradient_buffer[:, :, :, :cols_here]
        .at[:, :, :, : window_side - 1]
        .add(gradient_buffer[:, :, :, cols_here:])
    )
    pad_rows = (upper_count + 1) * rows_here - folded.shape[2]
    padded = jnp.pad(folded, ((0, 0), (0, 0), (0, pad_rows), (0, 0)))
    shares = [
        padded[:, :, offset * rows_here : (offset + 1) * rows_here]
        for offset in range(upper_count + 1)
    ]
    own_grad = shares[0]
    for offset in range(1, upper_count + 1):
        own_grad = own_grad + from_behind(shares[offset], "tile", offset)
    probe_grad = lax.psum(jnp.sum(probe_terms, axis=0), "tile")
    return (own_grad, probe_grad)


def solution(mesh):
    placed = (
        P(None, None, ("scan", "tile"), None),
        P("scan", None, None, None),
        P(("scan", "tile")),
        P(("scan", "tile")),
        P(("scan", "tile"), None, None),
    )
    return jax.shard_map(
        on_device,
        mesh=mesh,
        in_specs=placed,
        out_specs=(P(None, None, ("scan", "tile"), None), P("scan", None, None, None)),
        check_vma=False,
    )
```

profile of v0, /device:TPU:0, one launch (start us, length us, event | category | flops | bytes accessed | tf_op | source)
XLA Modules:
  0.0 459.3 jit_solution(3375297501975912838)
XLA Ops:
  7.2 5.5 %collective-permute-start = (f32[4,2,32,1024]{3,2,1,0:T(8,128)}, f32[4,2,32,1024]{3,2,1,0:T(8,128)S(1)}, u32[]{:S(2)}, u32[]{:S(2)}) collective-permute-start(f32[4,2,32,1024]{3,2,1,0:T(8,128)} %param.9), channel_id=1, source_target_pairs={{0,15},{1,0},{2,1},{3,2},{4,3},{5,4},{6,5},{7,6},{8,7},{9,8},{10,9... | collective-permute-start | bytes 3145736 | tf_op jit(solution)/shard_map/ppermute | solution.py:15
  12.7 12.6 %collective-permute-done = f32[4,2,32,1024]{3,2,1,0:T(8,128)S(1)} collective-permute-done((f32[4,2,32,1024]{3,2,1,0:T(8,128)}, f32[4,2,32,1024]{3,2,1,0:T(8,128)S(1)}, u32[]{:S(2)}, u32[]{:S(2)}) %collective-permute-start) | collective-permute-done | bytes 1048608 | tf_op jit(solution)/shard_map/ppermute | solution.py:15
  25.4 4.5 collective-permute-start.1
  29.9 12.3 %collective-permute-done.1 = f32[4,2,32,1024]{3,2,1,0:T(8,128)S(1)} collective-permute-done((f32[4,2,32,1024]{3,2,1,0:T(8,128)S(1)}, f32[4,2,32,1024]{3,2,1,0:T(8,128)S(1)}, u32[]{:S(2)}, u32[]{:S(2)}) %collective-permute-start.1) | collective-permute-done | bytes 1048608 | tf_op jit(solution)/shard_map/ppermute | solution.py:15
  42.2 4.6 %collective-permute-start.2 = (f32[4,2,32,1024]{3,2,1,0:T(8,128)S(1)}, f32[4,2,32,1024]{3,2,1,0:T(8,128)S(1)}, u32[]{:S(2)}, u32[]{:S(2)}) collective-permute-start(f32[4,2,32,1024]{3,2,1,0:T(8,128)S(1)} %collective-permute-done.1), channel_id=1, source_target_pairs={{0,15},{1,0},{2,1},{3,2},{4,3},{5,4},{6,5},{7,6},{8,7},{9,8},{10,9... | collective-permute-start | bytes 3145736 | tf_op jit(solution)/shard_map/ppermute | solution.py:15
  49.1 10.0 %collective-permute-done.2 = f32[4,2,32,1024]{3,2,1,0:T(8,128)S(1)} collective-permute-done((f32[4,2,32,1024]{3,2,1,0:T(8,128)S(1)}, f32[4,2,32,1024]{3,2,1,0:T(8,128)S(1)}, u32[]{:S(2)}, u32[]{:S(2)}) %collective-permute-start.2) | collective-permute-done | bytes 1048608 | tf_op jit(solution)/shard_map/ppermute | solution.py:15
  59.1 4.6 %collective-permute-start.3 = (f32[4,2,32,1024]{3,2,1,0:T(8,128)S(1)}, f32[4,2,32,1024]{3,2,1,0:T(8,128)}, u32[]{:S(2)}, u32[]{:S(2)}) collective-permute-start(f32[4,2,32,1024]{3,2,1,0:T(8,128)S(1)} %collective-permute-done.2), channel_id=1, source_target_pairs={{0,15},{1,0},{2,1},{3,2},{4,3},{5,4},{6,5},{7,6},{8,7},{9,8},{10,9... | collective-permute-start | bytes 3145736 | tf_op jit(solution)/shard_map/ppermute | solution.py:15
  64.6 1.3 constant_dynamic-update-slice_fusion.4
  67.2 8.8 %collective-permute-done.3 = f32[4,2,32,1024]{3,2,1,0:T(8,128)} collective-permute-done((f32[4,2,32,1024]{3,2,1,0:T(8,128)S(1)}, f32[4,2,32,1024]{3,2,1,0:T(8,128)}, u32[]{:S(2)}, u32[]{:S(2)}) %collective-permute-start.3) | collective-permute-done | bytes 1048608 | tf_op jit(solution)/shard_map/ppermute | solution.py:15
  76.0 1.3 constant_dynamic-update-slice_fusion
  77.4 3.2 pad_maximum_fusion
  80.6 17.6 %while.16 = (s32[]{:T(128)}, f32[4,2,159,1151]{3,2,1,0:T(8,128)}, s32[4,4]{1,0:T(4,128)S(1)}, f32[4,4,2,128,128]{4,3,2,1,0:T(8,128)}, s32[]{:T(128)}) while((s32[]{:T(128)}, f32[4,2,159,1151]{3,2,1,0:T(8,128)}, s32[4,4]{1,0:T(4,128)S(1)}, f32[4,4,2,128,128]{4,3,2,1,0:T(8,128)}, s32[]{:T(128)}) %tuple.92), condition=%wide.while_cond.1, body=%wide.while_body.1.sunk | while | flops 2 | bytes 1050225 | solution.py:114
  81.3 3.6 bitcast_dynamic-update-slice_fusion.2
  85.5 3.6 bitcast_dynamic-update-slice_fusion.2
  89.8 3.6 bitcast_dynamic-update-slice_fusion.2
  94.1 3.6 bitcast_dynamic-update-slice_fusion.2
  98.2 1.7 slice_bitcast_fusion.7
  110.4 1.4 fusion.38
  113.0 1.2 fusion.39
  122.3 1.4 fusion.36
  129.6 1.2 fusion.34
  132.0 1.2 fusion.35
  134.3 1.5 convolution_add_fusion.34
  146.3 1.4 fusion.88
  158.4 1.4 fusion.29
  170.7 1.3 fusion.25
  186.0 1.9 multiply_reduce_fusion.10
  196.4 1.2 fusion.11
  201.1 2.0 multiply_reduce_fusion.6
  216.9 2.2 add_bitcast_fusion.1
  222.5 1.2 add_bitcast_fusion.6
  226.1 3.0 broadcast_in_dim.12
  229.1 54.3 %while.15 = (s32[]{:T(128)}, f32[4,2,159,1151]{3,2,1,0:T(8,128)}, s32[4]{0:T(128)S(1)}, s32[4]{0:T(128)S(1)}, f32[4,4,2,128,128]{4,3,0,2,1:T(8,128)S(1)}, /*index=5*/s32[]{:T(128)}, s32[]{:T(128)}, s32[]{:T(128)}, s32[]{:T(128)}) while((s32[]{:T(128)}, f32[4,2,159,1151]{3,2,1,0:T(8,128)}, s32[4]{0:T(128)S(1)}, s32[4]{0:T(128)S(1)}, ...), condition=%wide.region_18.19_spmd, body=%wide.region_17.18_spmd.sunk | while | flops 131080 | bytes 2621641 | solution.py:124
  234.1 1.5 bitcast_add_fusion.2
  235.6 7.0 %dynamic_update_slice.8 = f32[4,2,159,1151]{3,2,1,0:T(8,128)} dynamic-update-slice(f32[4,2,159,1151]{3,2,1,0:T(8,128)} %get-tuple-element.289, f32[4,2,128,128]{3,2,1,0:T(8,128)S(1)} %bitcast_add_fusion.2, s32[]{:T(128)} %constant.98.clone.1..sunk, s32[]{:T(128)} %constant.98.clone.1..sunk, s32[]{:T(128)S(6)} %select_n.692, s32[]{:T(128)S(6)} %select_n.693) | dynamic-update-slice | bytes 1048580 | tf_op jit(solution)/shard_map/while/body/eval_jaxpr/dynamic_update_slice | solution.py:122
  247.6 1.5 bitcast_add_fusion.2
  249.1 7.1 %dynamic_update_slice.8 = f32[4,2,159,1151]{3,2,1,0:T(8,128)} dynamic-update-slice(f32[4,2,159,1151]{3,2,1,0:T(8,128)} %get-tuple-element.289, f32[4,2,128,128]{3,2,1,0:T(8,128)S(1)} %bitcast_add_fusion.2, s32[]{:T(128)} %constant.98.clone.1..sunk, s32[]{:T(128)} %constant.98.clone.1..sunk, s32[]{:T(128)S(6)} %select_n.692, s32[]{:T(128)S(6)} %select_n.693) | dynamic-update-slice | bytes 1048580 | tf_op jit(solution)/shard_map/while/body/eval_jaxpr/dynamic_update_slice | solution.py:122
  261.2 1.5 bitcast_add_fusion.2
  262.7 7.0 %dynamic_update_slice.8 = f32[4,2,159,1151]{3,2,1,0:T(8,128)} dynamic-update-slice(f32[4,2,159,1151]{3,2,1,0:T(8,128)} %get-tuple-element.289, f32[4,2,128,128]{3,2,1,0:T(8,128)S(1)} %bitcast_add_fusion.2, s32[]{:T(128)} %constant.98.clone.1..sunk, s32[]{:T(128)} %constant.98.clone.1..sunk, s32[]{:T(128)S(6)} %select_n.692, s32[]{:T(128)S(6)} %select_n.693) | dynamic-update-slice | bytes 1048580 | tf_op jit(solution)/shard_map/while/body/eval_jaxpr/dynamic_update_slice | solution.py:122
  274.8 1.5 bitcast_add_fusion.2
  276.3 7.0 %dynamic_update_slice.8 = f32[4,2,159,1151]{3,2,1,0:T(8,128)} dynamic-update-slice(f32[4,2,159,1151]{3,2,1,0:T(8,128)} %get-tuple-element.289, f32[4,2,128,128]{3,2,1,0:T(8,128)S(1)} %bitcast_add_fusion.2, s32[]{:T(128)} %constant.98.clone.1..sunk, s32[]{:T(128)} %constant.98.clone.1..sunk, s32[]{:T(128)S(6)} %select_n.692, s32[]{:T(128)S(6)} %select_n.693) | dynamic-update-slice | bytes 1048580 | tf_op jit(solution)/shard_map/while/body/eval_jaxpr/dynamic_update_slice | solution.py:122
  283.3 5.7 %slice.104 = f32[4,2,159,1024]{3,2,1,0:T(8,128)} slice(f32[4,2,159,1151]{3,2,1,0:T(8,128)} %get-tuple-element.108), slice={[0:4], [0:2], [0:159], [0:1024]} | slice | bytes 10420224 | tf_op jit(solution)/shard_map/slice | solution.py:128
  289.1 1.4 slice_add_fusion.1
  290.4 3.7 scatter-add.4
  294.1 4.1 fusion.846
  299.1 147.3 %all-reduce.13.cloned.1.call-done = f32[2,2,128,128]{2,3,0,1:T(8,128)} async-done(((f32[2,2,128,128]{2,3,0,1:T(8,128)}), f32[2,2,128,128]{2,3,0,1:T(8,128)}) %all-reduce.13.cloned.1.call-update) | async-done | bytes 262160 | tf_op jit(solution)/shard_map/psum | solution.py:141
  446.4 1.8 copy.344
  448.2 4.1 fusion.44
  (174 shorter events, 117.6 us)
Async XLA Ops:
  7.2 439.2 %all-reduce.13.cloned.1.call-start = ((), (), s32[]{:S(2)}) async-start(), calls=%async_computation | async-start | bytes 524288 | tf_op jit(solution)/shard_map/psum | solution.py:141
  7.2 18.2 %collective-permute-start = (f32[4,2,32,1024]{3,2,1,0:T(8,128)}, f32[4,2,32,1024]{3,2,1,0:T(8,128)S(1)}, u32[]{:S(2)}, u32[]{:S(2)}) collective-permute-start(f32[4,2,32,1024]{3,2,1,0:T(8,128)} %param.9), channel_id=1, source_target_pairs={{0,15},{1,0},{2,1},{3,2},{4,3},{5,4},{6,5},{7,6},{8,7},{9,8},{10,9... | collective-permute-start | bytes 3145736 | tf_op jit(solution)/shard_map/ppermute | solution.py:15
  25.4 16.8 %collective-permute-start.1 = (f32[4,2,32,1024]{3,2,1,0:T(8,128)S(1)}, f32[4,2,32,1024]{3,2,1,0:T(8,128)S(1)}, u32[]{:S(2)}, u32[]{:S(2)}) collective-permute-start(f32[4,2,32,1024]{3,2,1,0:T(8,128)S(1)} %collective-permute-done), channel_id=1, source_target_pairs={{0,15},{1,0},{2,1},{3,2},{4,3},{5,4},{6,5},{7,6},{8,7},{9,8},{10,9... | collective-permute-start | bytes 3145736 | tf_op jit(solution)/shard_map/ppermute | solution.py:15
  42.2 16.9 %collective-permute-start.2 = (f32[4,2,32,1024]{3,2,1,0:T(8,128)S(1)}, f32[4,2,32,1024]{3,2,1,0:T(8,128)S(1)}, u32[]{:S(2)}, u32[]{:S(2)}) collective-permute-start(f32[4,2,32,1024]{3,2,1,0:T(8,128)S(1)} %collective-permute-done.1), channel_id=1, source_target_pairs={{0,15},{1,0},{2,1},{3,2},{4,3},{5,4},{6,5},{7,6},{8,7},{9,8},{10,9... | collective-permute-start | bytes 3145736 | tf_op jit(solution)/shard_map/ppermute | solution.py:15
  59.1 16.9 %collective-permute-start.3 = (f32[4,2,32,1024]{3,2,1,0:T(8,128)S(1)}, f32[4,2,32,1024]{3,2,1,0:T(8,128)}, u32[]{:S(2)}, u32[]{:S(2)}) collective-permute-start(f32[4,2,32,1024]{3,2,1,0:T(8,128)S(1)} %collective-permute-done.2), channel_id=1, source_target_pairs={{0,15},{1,0},{2,1},{3,2},{4,3},{5,4},{6,5},{7,6},{8,7},{9,8},{10,9... | collective-permute-start | bytes 3145736 | tf_op jit(solution)/shard_map/ppermute | solution.py:15
  158.3 7.2 %copy-start.7 = (f32[4,128,128]{2,1,0:T(8,128)S(1)}, f32[4,128,128]{2,1,0:T(8,128)}, u32[]{:S(2)}) copy-start(f32[4,128,128]{2,1,0:T(8,128)} %param.13) | copy-start | bytes 786436
  219.0 4.7 %copy-start.1 = (f32[4,128,128]{2,1,0:T(8,128)S(1)}, f32[4,128,128]{2,1,0:T(8,128)}, u32[]{:S(2)}) copy-start(f32[4,128,128]{2,1,0:T(8,128)} %get-tuple-element.139) | copy-start | bytes 786436
  219.0 4.7 %copy-start.2 = (f32[4,128,128]{2,1,0:T(8,128)S(1)}, f32[4,128,128]{2,1,0:T(8,128)}, u32[]{:S(2)}) copy-start(f32[4,128,128]{2,1,0:T(8,128)} %get-tuple-element.140) | copy-start | bytes 786436
  219.0 4.7 %copy-start.3 = (f32[4,128,128]{2,1,0:T(8,128)S(1)}, f32[4,128,128]{2,1,0:T(8,128)}, u32[]{:S(2)}) copy-start(f32[4,128,128]{2,1,0:T(8,128)} %get-tuple-element.141) | copy-start | bytes 786436
  219.9 4.9 %copy-start.4 = (f32[4,128,128]{2,1,0:T(8,128)S(1)}, f32[4,128,128]{2,1,0:T(8,128)}, u32[]{:S(2)}) copy-start(f32[4,128,128]{2,1,0:T(8,128)} %copy.339) | copy-start | bytes 786436
  220.7 4.0 copy-start.5
  221.6 3.2 copy-start.6
  225.8 3.2 copy-start.8
  225.8 3.2 copy-start.9
  294.1 4.2 copy-start
  298.2 150.0 %collective-permute-start.4 = (f32[4,2,32,1024]{3,2,1,0:T(8,128)}, f32[4,2,32,1024]{3,2,1,0:T(8,128)}, u32[]{:S(2)}, u32[]{:S(2)}) collective-permute-start(f32[4,2,32,1024]{3,2,1,0:T(8,128)} %get-tuple-element.169), channel_id=1, source_target_pairs={{0,1},{1,2},{2,3},{3,4},{4,5},{5,6},{6,7},{7,8},{8,9},{9,10},{10,1... | collective-permute-start | bytes 3145736 | tf_op jit(solution)/shard_map/ppermute | solution.py:15
  298.2 150.0 %collective-permute-start.5 = (f32[4,2,32,1024]{3,2,1,0:T(8,128)}, f32[4,2,32,1024]{3,2,1,0:T(8,128)}, u32[]{:S(2)}, u32[]{:S(2)}) collective-permute-start(f32[4,2,32,1024]{3,2,1,0:T(8,128)} %get-tuple-element.172), channel_id=1, source_target_pairs={{0,2},{1,3},{2,4},{3,5},{4,6},{5,7},{6,8},{7,9},{8,10},{9,11},{10,... | collective-permute-start | bytes 3145736 | tf_op jit(solution)/shard_map/ppermute | solution.py:15
  298.2 150.0 %collective-permute-start.6 = (f32[4,2,32,1024]{3,2,1,0:T(8,128)S(1)}, f32[4,2,32,1024]{3,2,1,0:T(8,128)}, u32[]{:S(2)}, u32[]{:S(2)}) collective-permute-start(f32[4,2,32,1024]{3,2,1,0:T(8,128)S(1)} %get-tuple-element.171), channel_id=1, source_target_pairs={{0,3},{1,4},{2,5},{3,6},{4,7},{5,8},{6,9},{7,10},{8,11},{9,12},{10... | collective-permute-start | bytes 3145736 | tf_op jit(solution)/shard_map/ppermute | solution.py:15
  298.3 149.9 %collective-permute-start.7 = (f32[4,2,32,1024]{3,2,1,0:T(8,128)S(1)}, f32[4,2,32,1024]{3,2,1,0:T(8,128)}, u32[]{:S(2)}, u32[]{:S(2)}) collective-permute-start(f32[4,2,32,1024]{3,2,1,0:T(8,128)S(1)} %get-tuple-element.170), channel_id=1, source_target_pairs={{0,4},{1,5},{2,6},{3,7},{4,8},{5,9},{6,10},{7,11},{8,12},{9,13},{1... | collective-permute-start | bytes 3145736 | tf_op jit(solution)/shard_map/ppermute | solution.py:15
Sparse Core Ops, SparseCore 0:
  299.2 147.1 all-reduce.12
where the time goes:
time: 464 us; the launch traced here: 459 us
  waiting for transfers between devices  191 us (41%)
  matrix products  118 us (25%)
  local copies, waits for them, and re-layouts  78.3 us (17%)
  other arithmetic  21.3 us (5%)
  starting transfers between devices  19.4 us (4%)
  loops' own time  16 us (3%)
  between operations  15.3 us (3%)
    psum x1, waiting for transfers between devices, on_device(): probe_grad = lax.psum(jnp.sum(probe_terms, axis=0), 'tile')  147 us
    dot_general x56, matrix products, product(): jnp.einsum('jk,mkl->mjl', matrix, field, precision=lax.Precision.HIGHEST)  62.3 us
    dot_general x56, matrix products, product(): jnp.einsum('mjk,kl->mjl', field, matrix, precision=lax.Precision.HIGHEST)  55.7 us
    ppermute x8, waiting for transfers between devices, from_behind(): return lax.ppermute(value, axis, pairs)  43.8 us
    dynamic_update_slice x4, local copies, waits for them, and re-layouts, add_window(): lax.dynamic_update_slice(gradient_buffer, current + crop_grads[window_ind...  28.1 us
    ppermute x8, starting transfers between devices, from_behind(): return lax.ppermute(value, axis, pairs)  19.4 us
    gather x12, local copies, waits for them, and re-layouts  17.1 us
    another operation x1, loops' own time, on_device(): lax.fori_loop(0, row_offset.shape[0], add_window, jnp.zeros(extended.shap...  15.6 us
  transfers between devices with their start and end apart: 9, of which 5 were waited for; matrix products, arithmetic and copies ran while one was open for 2% of the time, Pallas kernels for 0%

commit v1 on v0

v1 whole, which is shorter than its diff:
```python
import functools
import math

import jax
import jax.numpy as jnp
import numpy as np
from jax import lax
from jax.experimental import pallas as pl
from jax.experimental.pallas import tpu as pltpu
from jax.sharding import PartitionSpec as P

INTENSITY_SHIFT = 0.5
FRESNEL = 0.75
LANES = 128
SUBLANES = 8


def field_tables(side):
    idx = np.arange(side)
    fourier = np.exp(-2j * np.pi * (np.outer(idx, idx) % side) / side) / np.sqrt(side)
    freq = (idx + side // 2) % side - side // 2
    line = np.exp(-1j * np.pi * FRESNEL * freq**2 / (side / 2.0) ** 2)
    propagator = fourier.conj() @ (line[:, None] * fourier)
    blocks = []
    for matrix in (propagator, fourier, fourier.conj(), propagator.conj()):
        block = np.block([[matrix.real, matrix.imag], [-matrix.imag, matrix.real]])
        high = block.astype(np.float32).astype(jnp.bfloat16)
        low = (block - high.astype(np.float64)).astype(np.float32).astype(jnp.bfloat16)
        blocks.append(np.stack([high, low]))
    return np.stack(blocks)


PROP, FWD, INV, PROP_ADJ = range(4)
CONJ = {PROP: PROP_ADJ, FWD: INV, INV: FWD, PROP_ADJ: PROP}


def split_pair(value):
    high = value.astype(jnp.bfloat16)
    low = (value - high.astype(jnp.float32)).astype(jnp.bfloat16)
    return high, low


def two_sided(table_ref, which, fields, side):
    right_high, right_low = table_ref[which, 0], table_ref[which, 1]
    right_mat = jnp.concatenate([right_high, right_low, right_high], axis=0)
    halves = []
    for modes in fields:
        rows = jnp.concatenate([jnp.concatenate([re, im], axis=1) for re, im in modes], axis=0)
        high, low = split_pair(rows)
        lhs = jnp.concatenate([high, high, low], axis=1)
        halves.append(jnp.dot(lhs, right_mat, preferred_element_type=jnp.float32))
    left_high, left_low = table_ref[CONJ[which], 0], table_ref[CONJ[which], 1]
    left_mat = jnp.concatenate([left_high, left_high, left_low], axis=1)
    results = []
    for half, modes in zip(halves, fields):
        count = len(modes)
        high, low = split_pair(half)

        def stack(part):
            pieces = [part[m * side : (m + 1) * side] for m in range(count)]
            return jnp.concatenate(
                [
                    jnp.concatenate([p[:, :side] for p in pieces], axis=1),
                    jnp.concatenate([p[:, side:] for p in pieces], axis=1),
                ],
                axis=0,
            )

        high, low = stack(high), stack(low)
        rhs = jnp.concatenate([high, low, high], axis=0)
        full = jnp.dot(left_mat, rhs, preferred_element_type=jnp.float32)
        results.append(
            [
                (full[:side, m * side : (m + 1) * side], full[side:, m * side : (m + 1) * side])
                for m in range(count)
            ]
        )
    return results


def window_kernel(pieces_count, row_ref, col_ref, *refs):
    pieces = refs[:pieces_count]
    probe_ref, amp_ref, table_ref = refs[pieces_count : pieces_count + 3]
    outs = refs[pieces_count + 3 : 2 * pieces_count + 3]
    probe_out = refs[2 * pieces_count + 3]
    ext, grad, crops, waves, in_sem, out_sem = refs[2 * pieces_count + 4 :]
    slice_count, _, rows_here, cols_here = pieces[0].shape
    windows, side = amp_ref.shape[0], amp_ref.shape[1]
    modes = probe_ref.shape[0]
    col_blocks = cols_here // LANES

    def incoming(s, o):
        return pltpu.make_async_copy(
            pieces[o].at[s], ext.at[s, :, pl.ds(o * rows_here, rows_here)], in_sem.at[s, o]
        )

    def outgoing(s, o):
        return pltpu.make_async_copy(
            grad.at[s, :, pl.ds(o * rows_here, rows_here)], outs[o].at[s], out_sem.at[s, o]
        )

    for s in range(slice_count):
        for o in range(pieces_count):
            incoming(s, o).start()
    grad[...] = jnp.zeros_like(grad)

    tall = side + SUBLANES
    lane = lax.broadcasted_iota(jnp.int32, (tall, LANES), 1)
    margin = jnp.zeros((SUBLANES, LANES), jnp.float32)
    places = []
    for w in range(windows):
        row, col = row_ref[w], col_ref[w]
        block = col // LANES
        shift = col - block * LANES
        first = pl.multiple_of(block * LANES, LANES)
        second = pl.multiple_of(lax.rem(block + 1, col_blocks) * LANES, LANES)
        base = row // SUBLANES * SUBLANES
        places.append((pl.multiple_of(base, SUBLANES), row - base, first, second, shift))

    fields = [[(probe_ref[m, 0], probe_ref[m, 1]) for m in range(modes)] for _ in range(windows)]
    for s in range(slice_count):
        for o in range(pieces_count):
            incoming(s, o).wait()
        exits = []
        for w in range(windows):
            row, lift, first, second, shift = places[w]
            back = lax.rem(LANES - shift, LANES)
            planes = []
            for c in range(2):
                one = pltpu.roll(ext[s, c, pl.ds(row, tall), pl.ds(first, LANES)], back, 1)
                two = pltpu.roll(ext[s, c, pl.ds(row, tall), pl.ds(second, LANES)], back, 1)
                plane = jnp.where(lane < LANES - shift, one, two)
                plane = pltpu.roll(plane, lax.rem(tall - lift, tall), 0)[:side]
                crops[s, w, c] = plane
                planes.append(plane)
            obj_re, obj_im = planes
            chi = []
            for m in range(modes):
                re, im = fields[w][m]
                chi.append((obj_re * re - obj_im * im, obj_re * im + obj_im * re))
            exits.append(chi)
        fields = two_sided(table_ref, PROP if s + 1 < slice_count else FWD, exits, side)
        if s + 1 < slice_count:
            for w in range(windows):
                for m in range(modes):
                    waves[s, w, m, 0] = fields[w][m][0]
                    waves[s, w, m, 1] = fields[w][m][1]

    far_grads = []
    for w in range(windows):
        intensity = sum(re * re + im * im for re, im in fields[w])
        factor = 1.0 - amp_ref[w] / jnp.sqrt(intensity + INTENSITY_SHIFT)
        far_grads.append([(factor * re, factor * im) for re, im in fields[w]])
    fields = two_sided(table_ref, INV, far_grads, side)

    for s in reversed(range(slice_count)):
        wave_grads = []
        for w in range(windows):
            row, lift, first, second, shift = places[w]
            obj_re, obj_im = crops[s, w, 0], crops[s, w, 1]
            grad_re = jnp.zeros((side, side), jnp.float32)
            grad_im = jnp.zeros((side, side), jnp.float32)
            terms = []
            for m in range(modes):
                re, im = fields[w][m]
                if s == 0:
                    wave_re, wave_im = probe_ref[m, 0], probe_ref[m, 1]
                else:
                    wave_re, wave_im = waves[s - 1, w, m, 0], waves[s - 1, w, m, 1]
                grad_re += re * wave_re + im * wave_im
                grad_im += im * wave_re - re * wave_im
                terms.append((re * obj_re + im * obj_im, im * obj_re - re * obj_im))
            wave_grads.append(terms)
            for c, plane in enumerate((grad_re, grad_im)):
                turned = pltpu.roll(jnp.concatenate([plane, margin], axis=0), lift, 0)
                turned = pltpu.roll(turned, shift, 1)
                low = jnp.where(lane >= shift, turned, 0.0)
                grad[s, c, pl.ds(row, tall), pl.ds(first, LANES)] += low
                high = jnp.where(lane < shift, turned, 0.0)
                grad[s, c, pl.ds(row, tall), pl.ds(second, LANES)] += high
        for o in range(pieces_count):
            outgoing(s, o).start()
        if s > 0:
            fields = two_sided(table_ref, PROP_ADJ, wave_grads, side)
    for m in range(modes):
        for c in range(2):
            probe_out[m, c] = sum(wave_grads[w][m][c] for w in range(windows))
    for s in range(slice_count):
        for o in range(pieces_count):
            outgoing(s, o).wait()


def run_windows(pieces, probe_modes, row_offset, col_offset, amplitude):
    count = len(pieces)
    slice_count, parts, rows_here, cols_here = pieces[0].shape
    windows, side = amplitude.shape[0], amplitude.shape[1]
    modes = probe_modes.shape[0]
    tables = jnp.asarray(field_tables(side))
    anywhere = pl.BlockSpec(memory_space=pl.ANY)
    vmem = pl.BlockSpec(memory_space=pltpu.VMEM)
    smem = pl.BlockSpec(memory_space=pltpu.SMEM)
    total = count * rows_here
    return pl.pallas_call(
        functools.partial(window_kernel, count),
        out_shape=[jax.ShapeDtypeStruct(p.shape, jnp.float32) for p in pieces]
        + [jax.ShapeDtypeStruct(probe_modes.shape, jnp.float32)],
        in_specs=[smem, smem] + [anywhere] * count + [vmem] * 3,
        out_specs=[anywhere] * count + [vmem],
        scratch_shapes=[
            pltpu.VMEM((slice_count, parts, total, cols_here), jnp.float32),
            pltpu.VMEM((slice_count, parts, total, cols_here), jnp.float32),
            pltpu.VMEM((slice_count, windows, parts, side, side), jnp.float32),
            pltpu.VMEM((slice_count - 1, windows, modes, 2, side, side), jnp.float32),
            pltpu.SemaphoreType.DMA((slice_count, count)),
            pltpu.SemaphoreType.DMA((slice_count, count)),
        ],
        compiler_params=pltpu.CompilerParams(vmem_limit_bytes=48 << 20),
        name="windows",
    )(row_offset, col_offset, *pieces, probe_modes, amplitude, tables)


def permute(value, pairs):
    return lax.ppermute(value, "tile", pairs)


def on_device(slices, probe_modes, row_offset, col_offset, amplitude):
    side = probe_modes.shape[-1]
    rows_here = slices.shape[2]
    reach = (side - 2) // rows_here + 1
    assert reach == 4
    tiles = lax.axis_size("tile")
    index = lax.axis_index("tile")
    core = index % 2
    odd_chip = (index // 2) % 2
    swap_core = [(s, s ^ 1) for s in range(tiles)]
    swap_chip = [(s, s ^ 2) for s in range(tiles)]
    ahead = [(s, (s - 4) % tiles) for s in range(tiles)]
    behind = [(s, (s + 4) % tiles) for s in range(tiles)]

    fourth = permute(slices, ahead)
    second = permute(jnp.where(odd_chip == 1, slices, fourth), swap_chip)
    first = permute(jnp.where(core == 1, slices, second), swap_core)
    third = permute(jnp.where(core == 1, second, fourth), swap_core)
    pieces = [slices, first, second, third, fourth]

    *shares, probe_terms = run_windows(pieces, probe_modes, row_offset, col_offset, amplitude)

    got_first = permute(shares[1], swap_core)
    got_third = permute(shares[3], swap_core)
    low_core = core == 0
    sum_second = shares[2] + jnp.where(low_core, got_first, got_third)
    got_second = permute(sum_second, swap_chip)
    even = odd_chip == 0
    sum_fourth = shares[4] + jnp.where(low_core, got_third, 0.0) + jnp.where(even, got_second, 0.0)
    own = shares[0] + jnp.where(low_core, 0.0, got_first) + jnp.where(even, 0.0, got_second)
    slice_grad = own + permute(sum_fourth, behind)

    step = 1
    while step < tiles:
        probe_terms = probe_terms + permute(probe_terms, [(s, s ^ step) for s in range(tiles)])
        step *= 2
    return (slice_grad, probe_terms)


def solution(mesh):
    placed = (
        P(None, None, ("scan", "tile"), None),
        P("scan", None, None, None),
        P(("scan", "tile")),
        P(("scan", "tile")),
        P(("scan", "tile"), None, None),
    )
    return jax.shard_map(
        on_device,
        mesh=mesh,
        in_specs=placed,
        out_specs=(P(None, None, ("scan", "tile"), None), P("scan", None, None, None)),
        check_vma=False,
    )
```

time: 464 us -> 159 us (0.34)
  matrix products: 118 us -> 0 us
  local copies, waits for them, and re-layouts: 78.3 us -> 1.7 us
  waiting for transfers between devices: 191 us -> 117 us
  loops' own time: 16 us -> 0 us
  Pallas kernels: 0 us -> 15.6 us
  between operations: 15.3 us -> 0.68 us
  other arithmetic: 21.3 us -> 7.76 us
    psum x1 -> x0, waiting for transfers between devices: 147 us -> none  [on_device(): probe_grad = lax.psum(jnp.sum(probe_terms, axis=0), 'tile')]
    dot_general x112 -> x0, matrix products: 118 us -> none  [the longest x56 62.3 us: product(): jnp.einsum('jk,mkl->mjl', matrix, field, precision=lax.Precision.HIGHEST)]
    ppermute x8 -> x12, waiting for transfers between devices: 43.8 us -> 117 us  [permute(): return lax.ppermute(value, 'tile', pairs)]
    dynamic_update_slice x4 -> x0, local copies, waits for them, and re-layouts: 28.1 us -> none  [add_window(): lax.dynamic_update_slice(gradient_buffer, current + crop_grads[window_ind...]
    gather x12 -> x0, local copies, waits for them, and re-layouts: 17.1 us -> none
    another operation x2 -> x0, loops' own time: 16 us -> none  [the longest x1 15.6 us: on_device(): lax.fori_loop(0, row_offset.shape[0], add_window, jnp.zeros(extended.shap...]
    pallas_call x0 -> x1, Pallas kernels: none -> 15.6 us  [run_windows(): pl.pallas_call(functools.partial(window_kernel, count), out_shape=[jax.Sh...]
    slice x3 -> x0, local copies, waits for them, and re-layouts: 9.88 us -> none  [the longest x1 5.73 us: on_device(): gradient_buffer[:, :, :, :cols_here].at[:, :, :, :window_side - 1]]
  transfers between devices with their start and end apart: 9 -> 12, of which waited for: 5 -> 10; matrix products, arithmetic and copies ran while one was open for 2% -> 2% of each run, Pallas kernels for 0% -> 0%
where the time goes in v1:
time: 159 us; the launch traced here: 158 us
  waiting for transfers between devices  117 us (74%)
  Pallas kernels  15.6 us (10%)
  starting transfers between devices  15.4 us (10%)
  other arithmetic  7.76 us (5%)
  local copies, waits for them, and re-layouts  1.7 us (1%)
    ppermute x12, waiting for transfers between devices, permute(): return lax.ppermute(value, 'tile', pairs)  117 us
    pallas_call x1, Pallas kernels, run_windows(): pl.pallas_call(functools.partial(window_kernel, count), out_shape=[jax.Sh...  15.6 us
    ppermute x12, starting transfers between devices, permute(): return lax.ppermute(value, 'tile', pairs)  15.4 us
  transfers between devices with their start and end apart: 12, of which 10 were waited for; matrix products, arithmetic and copies ran while one was open for 2% of the time, Pallas kernels for 0%

profile of v1, /device:TPU:0, one launch (start us, length us, event | category | flops | bytes accessed | tf_op | source)
XLA Modules:
  0.0 158.2 jit_solution(14582650108119347662)
XLA Ops:
  0.6 5.1 %collective-permute-start = (f32[4,2,32,1024]{3,2,1,0:T(8,128)}, f32[4,2,32,1024]{3,2,1,0:T(8,128)S(1)}, u32[]{:S(2)}, u32[]{:S(2)}) collective-permute-start(f32[4,2,32,1024]{3,2,1,0:T(8,128)} %refs_0_.1), channel_id=1, source_target_pairs={{0,12},{1,13},{2,14},{3,15},{4,0},{5,1},{6,2},{7,3},{8,4},{9,5},{1... | collective-permute-start | bytes 3145736 | tf_op jit(solution)/shard_map/ppermute | solution.py:223
  5.8 0.0 copy-start.4
  5.8 22.7 %collective-permute-done.refs_4_ = f32[4,2,32,1024]{3,2,1,0:T(8,128)S(1)} collective-permute-done((f32[4,2,32,1024]{3,2,1,0:T(8,128)}, f32[4,2,32,1024]{3,2,1,0:T(8,128)S(1)}, u32[]{:S(2)}, u32[]{:S(2)}) %collective-permute-start) | collective-permute-done | bytes 1048608 | tf_op jit(solution)/shard_map/ppermute | solution.py:223
  28.5 0.0 copy-start.5
  28.5 1.2 broadcast_select_fusion
  29.7 3.0 %collective-permute-start.1 = (f32[4,2,32,1024]{3,2,1,0:T(8,128)}, f32[4,2,32,1024]{3,2,1,0:T(8,128)S(1)}, u32[]{:S(2)}, u32[]{:S(2)}) collective-permute-start(f32[4,2,32,1024]{3,2,1,0:T(8,128)} %broadcast_select_fusion), channel_id=1, source_target_pairs={{0,2},{1,3},{2,0},{3,1},{4,6},{5,7},{6,4},{7,5},{8,10},{9,11},{10,... | collective-permute-start | bytes 3145736 | tf_op jit(solution)/shard_map/ppermute | solution.py:223
  32.7 0.0 copy-start
  32.7 0.0 copy-start.1
  32.7 22.5 %collective-permute-done.1.refs_2_ = f32[4,2,32,1024]{3,2,1,0:T(8,128)S(1)} collective-permute-done((f32[4,2,32,1024]{3,2,1,0:T(8,128)}, f32[4,2,32,1024]{3,2,1,0:T(8,128)S(1)}, u32[]{:S(2)}, u32[]{:S(2)}) %collective-permute-start.1) | collective-permute-done | bytes 1048608 | tf_op jit(solution)/shard_map/ppermute | solution.py:223
  55.2 0.0 copy-done.5
  55.2 0.0 copy-done.4
  55.2 0.0 copy-start.6
  55.2 0.3 broadcast_select_fusion.1
  55.5 0.7 copy-done.6
  56.2 0.0 copy-start.2
  56.2 0.0 copy-start.3
  56.2 0.0 collective-permute-start.3
  56.2 0.5 collective-permute-start.2
  56.7 2.1 %collective-permute-done.3.refs_3_ = f32[4,2,32,1024]{3,2,1,0:T(8,128)S(1)} collective-permute-done((f32[4,2,32,1024]{3,2,1,0:T(8,128)S(1)}, f32[4,2,32,1024]{3,2,1,0:T(8,128)S(1)}, u32[]{:S(2)}, u32[]{:S(2)}) %collective-permute-start.3) | collective-permute-done | bytes 1048608 | tf_op jit(solution)/shard_map/ppermute | solution.py:223
  58.9 1.5 collective-permute-done.2.refs_1_
  60.4 0.0 copy-done.7
  60.4 0.0 copy-start.8
  60.4 1.0 copy-done.8
  61.4 0.0 copy-done
  61.4 0.0 copy-done.1
  61.4 0.0 copy-done.2
  61.4 0.0 copy-done.3
  61.4 15.6 %windows.1 = (f32[4,2,32,1024]{3,2,1,0:T(8,128)S(1)}, f32[4,2,32,1024]{3,2,1,0:T(8,128)}, f32[4,2,32,1024]{3,2,1,0:T(8,128)S(1)}, f32[4,2,32,1024]{3,2,1,0:T(8,1...) custom-call(s32[4]{0:T(128)S(1)} %copy-done.2, s32[4]{0:T(128)S(1)} %copy-done.3, ...), custom_call_target="tpu_custom_call" | custom-call | tf_op jit(solution)/shard_map/windows/pallas_call | solution.py:203
  77.0 0.2 collective-permute-start.4
  77.2 0.4 collective-permute-start.5
  77.6 2.5 %collective-permute-done.4 = f32[4,2,32,1024]{3,2,1,0:T(8,128)} collective-permute-done((f32[4,2,32,1024]{3,2,1,0:T(8,128)}, f32[4,2,32,1024]{3,2,1,0:T(8,128)}, u32[]{:S(2)}, u32[]{:S(2)}) %collective-permute-start.4) | collective-permute-done | bytes 1048608 | tf_op jit(solution)/shard_map/ppermute | solution.py:223
  80.1 1.5 collective-permute-done.5
  81.6 2.5 %select_add_fusion.1 = f32[4,2,32,1024]{3,2,1,0:T(8,128)} fusion(f32[4,2,32,1024]{3,2,1,0:T(8,128)S(1)} %get-tuple-element.10, f32[4,2,32,1024]{3,2,1,0:T(8,128)} %collective-permute-done.4, f32[4,2,32,1024]{3,2,1,0:T(8,128)} %collective-permute-done.5, pred[]{:T(512)S(6)} %eq.18), kind=kLoop, calls=%fused_computation.2 | loop fusion | flops 524288 | bytes 4194305 | tf_op jit(solution)/shard_map/add | solution.py:251
  84.1 1.7 %collective-permute-start.6 = (f32[4,2,32,1024]{3,2,1,0:T(8,128)}, f32[4,2,32,1024]{3,2,1,0:T(8,128)S(1)}, u32[]{:S(2)}, u32[]{:S(2)}) collective-permute-start(f32[4,2,32,1024]{3,2,1,0:T(8,128)} %select_add_fusion.1), channel_id=1, source_target_pairs={{0,2},{1,3},{2,0},{3,1},{4,6},{5,7},{6,4},{7,5},{8,10},{9,11},{10,... | collective-permute-start | bytes 3145736 | tf_op jit(solution)/shard_map/ppermute | solution.py:223
  85.8 0.0 collective-permute-start.8
  85.8 23.7 %collective-permute-done.6 = f32[4,2,32,1024]{3,2,1,0:T(8,128)S(1)} collective-permute-done((f32[4,2,32,1024]{3,2,1,0:T(8,128)}, f32[4,2,32,1024]{3,2,1,0:T(8,128)S(1)}, u32[]{:S(2)}, u32[]{:S(2)}) %collective-permute-start.6) | collective-permute-done | bytes 1048608 | tf_op jit(solution)/shard_map/ppermute | solution.py:223
  109.5 1.5 select_add_fusion
  111.0 0.4 collective-permute-start.7
  111.4 0.0 collective-permute-done.8
  111.5 1.8 %collective-permute-start.9 = (f32[2,2,128,128]{3,2,1,0:T(8,128)S(1)}, f32[2,2,128,128]{3,2,1,0:T(8,128)S(1)}, u32[]{:S(2)}, u32[]{:S(2)}) collective-permute-start(f32[2,2,128,128]{3,2,1,0:T(8,128)S(1)} %add.46), channel_id=1, source_target_pairs={{0,2},{1,3},{2,0},{3,1},{4,6},{5,7},{6,4},{7,5},{8,10},{9,11},{10,... | collective-permute-start | bytes 786440 | tf_op jit(solution)/shard_map/ppermute | solution.py:223
  113.3 4.6 %collective-permute-done.9 = f32[2,2,128,128]{3,2,1,0:T(8,128)S(1)} collective-permute-done((f32[2,2,128,128]{3,2,1,0:T(8,128)S(1)}, f32[2,2,128,128]{3,2,1,0:T(8,128)S(1)}, u32[]{:S(2)}, u32[]{:S(2)}) %collective-permute-start.9) | collective-permute-done | bytes 262176 | tf_op jit(solution)/shard_map/ppermute | solution.py:223
  117.9 1.6 %collective-permute-start.10 = (f32[2,2,128,128]{3,2,1,0:T(8,128)S(1)}, f32[2,2,128,128]{3,2,1,0:T(8,128)S(1)}, u32[]{:S(2)}, u32[]{:S(2)}) collective-permute-start(f32[2,2,128,128]{3,2,1,0:T(8,128)S(1)} %add.47), channel_id=1, source_target_pairs={{0,4},{1,5},{2,6},{3,7},{4,0},{5,1},{6,2},{7,3},{8,12},{9,13},{10,... | collective-permute-start | bytes 786440 | tf_op jit(solution)/shard_map/ppermute | solution.py:223
  119.6 22.7 %collective-permute-done.10 = f32[2,2,128,128]{3,2,1,0:T(8,128)S(1)} collective-permute-done((f32[2,2,128,128]{3,2,1,0:T(8,128)S(1)}, f32[2,2,128,128]{3,2,1,0:T(8,128)S(1)}, u32[]{:S(2)}, u32[]{:S(2)}) %collective-permute-start.10) | collective-permute-done | bytes 262176 | tf_op jit(solution)/shard_map/ppermute | solution.py:223
  142.3 0.6 collective-permute-start.11
  142.9 13.2 %collective-permute-done.11 = f32[2,2,128,128]{3,2,1,0:T(8,128)S(1)} collective-permute-done((f32[2,2,128,128]{3,2,1,0:T(8,128)S(1)}, f32[2,2,128,128]{3,2,1,0:T(8,128)S(1)}, u32[]{:S(2)}, u32[]{:S(2)}) %collective-permute-start.11) | collective-permute-done | bytes 262176 | tf_op jit(solution)/shard_map/ppermute | solution.py:223
  156.1 0.7 add.49
  156.8 0.0 collective-permute-done.7
  156.8 1.4 add_add_fusion
  (4 shorter events, 0.1 us)
Async XLA Ops:
  0.6 27.9 %collective-permute-start = (f32[4,2,32,1024]{3,2,1,0:T(8,128)}, f32[4,2,32,1024]{3,2,1,0:T(8,128)S(1)}, u32[]{:S(2)}, u32[]{:S(2)}) collective-permute-start(f32[4,2,32,1024]{3,2,1,0:T(8,128)} %refs_0_.1), channel_id=1, source_target_pairs={{0,12},{1,13},{2,14},{3,15},{4,0},{5,1},{6,2},{7,3},{8,4},{9,5},{1... | collective-permute-start | bytes 3145736 | tf_op jit(solution)/shard_map/ppermute | solution.py:223
  5.8 49.5 %copy-start.4 = (f32[4,2,32,1024]{3,2,1,0:T(8,128)S(1)}, f32[4,2,32,1024]{3,2,1,0:T(8,128)}, u32[]{:S(2)}) copy-start(f32[4,2,32,1024]{3,2,1,0:T(8,128)} %refs_0_.1) | copy-start | bytes 3145732
  28.5 26.8 %copy-start.5 = (f32[4,2,32,1024]{3,2,1,0:T(8,128)}, f32[4,2,32,1024]{3,2,1,0:T(8,128)S(1)}, u32[]{:S(2)}) copy-start(f32[4,2,32,1024]{3,2,1,0:T(8,128)S(1)} %collective-permute-done.refs_4_) | copy-start | bytes 3145732
  29.7 25.5 %collective-permute-start.1 = (f32[4,2,32,1024]{3,2,1,0:T(8,128)}, f32[4,2,32,1024]{3,2,1,0:T(8,128)S(1)}, u32[]{:S(2)}, u32[]{:S(2)}) collective-permute-start(f32[4,2,32,1024]{3,2,1,0:T(8,128)} %broadcast_select_fusion), channel_id=1, source_target_pairs={{0,2},{1,3},{2,0},{3,1},{4,6},{5,7},{6,4},{7,5},{8,10},{9,11},{10,... | collective-permute-start | bytes 3145736 | tf_op jit(solution)/shard_map/ppermute | solution.py:223
  32.7 28.6 %copy-start = (f32[2,2,128,128]{3,2,1,0:T(8,128)S(1)}, f32[2,2,128,128]{3,2,1,0:T(8,128)}, u32[]{:S(2)}) copy-start(f32[2,2,128,128]{3,2,1,0:T(8,128)} %refs_5_.1) | copy-start | bytes 786436
  32.7 28.6 %copy-start.1 = (f32[4,128,128]{2,1,0:T(8,128)S(1)}, f32[4,128,128]{2,1,0:T(8,128)}, u32[]{:S(2)}) copy-start(f32[4,128,128]{2,1,0:T(8,128)} %refs_6_.1) | copy-start | bytes 786436
  55.2 1.0 copy-start.6
  56.2 5.1 %copy-start.2 = (s32[4]{0:T(128)S(1)}, s32[4]{0:T(128)}, u32[]{:S(2)}) copy-start(s32[4]{0:T(128)} %row_ref.1) | copy-start | bytes 52
  56.2 5.1 %copy-start.3 = (s32[4]{0:T(128)S(1)}, s32[4]{0:T(128)}, u32[]{:S(2)}) copy-start(s32[4]{0:T(128)} %col_ref.1) | copy-start | bytes 52
  56.2 2.7 %collective-permute-start.3 = (f32[4,2,32,1024]{3,2,1,0:T(8,128)S(1)}, f32[4,2,32,1024]{3,2,1,0:T(8,128)S(1)}, u32[]{:S(2)}, u32[]{:S(2)}) collective-permute-start(f32[4,2,32,1024]{3,2,1,0:T(8,128)S(1)} %get-tuple-element.14), channel_id=1, source_target_pairs={{0,1},{1,0},{2,3},{3,2},{4,5},{5,4},{6,7},{7,6},{8,9},{9,8},{10,11... | collective-permute-start | bytes 3145736 | tf_op jit(solution)/shard_map/ppermute | solution.py:223
  56.2 4.2 %collective-permute-start.2 = (f32[4,2,32,1024]{3,2,1,0:T(8,128)S(1)}, f32[4,2,32,1024]{3,2,1,0:T(8,128)S(1)}, u32[]{:S(2)}, u32[]{:S(2)}) collective-permute-start(f32[4,2,32,1024]{3,2,1,0:T(8,128)S(1)} %get-tuple-element.15), channel_id=1, source_target_pairs={{0,1},{1,0},{2,3},{3,2},{4,5},{5,4},{6,7},{7,6},{8,9},{9,8},{10,11... | collective-permute-start | bytes 3145736 | tf_op jit(solution)/shard_map/ppermute | solution.py:223
  58.9 1.5 copy-start.7
  60.4 1.0 copy-start.8
  77.0 3.1 %collective-permute-start.4 = (f32[4,2,32,1024]{3,2,1,0:T(8,128)}, f32[4,2,32,1024]{3,2,1,0:T(8,128)}, u32[]{:S(2)}, u32[]{:S(2)}) collective-permute-start(f32[4,2,32,1024]{3,2,1,0:T(8,128)} %get-tuple-element.9), channel_id=1, source_target_pairs={{0,1},{1,0},{2,3},{3,2},{4,5},{5,4},{6,7},{7,6},{8,9},{9,8},{10,11... | collective-permute-start | bytes 3145736 | tf_op jit(solution)/shard_map/ppermute | solution.py:223
  77.2 4.4 %collective-permute-start.5 = (f32[4,2,32,1024]{3,2,1,0:T(8,128)}, f32[4,2,32,1024]{3,2,1,0:T(8,128)}, u32[]{:S(2)}, u32[]{:S(2)}) collective-permute-start(f32[4,2,32,1024]{3,2,1,0:T(8,128)} %get-tuple-element.11), channel_id=1, source_target_pairs={{0,1},{1,0},{2,3},{3,2},{4,5},{5,4},{6,7},{7,6},{8,9},{9,8},{10,11... | collective-permute-start | bytes 3145736 | tf_op jit(solution)/shard_map/ppermute | solution.py:223
  84.1 25.4 %collective-permute-start.6 = (f32[4,2,32,1024]{3,2,1,0:T(8,128)}, f32[4,2,32,1024]{3,2,1,0:T(8,128)S(1)}, u32[]{:S(2)}, u32[]{:S(2)}) collective-permute-start(f32[4,2,32,1024]{3,2,1,0:T(8,128)} %select_add_fusion.1), channel_id=1, source_target_pairs={{0,2},{1,3},{2,0},{3,1},{4,6},{5,7},{6,4},{7,5},{8,10},{9,11},{10,... | collective-permute-start | bytes 3145736 | tf_op jit(solution)/shard_map/ppermute | solution.py:223
  85.8 25.6 %collective-permute-start.8 = (f32[2,2,128,128]{3,2,1,0:T(8,128)S(1)}, f32[2,2,128,128]{3,2,1,0:T(8,128)S(1)}, u32[]{:S(2)}, u32[]{:S(2)}) collective-permute-start(f32[2,2,128,128]{3,2,1,0:T(8,128)S(1)} %get-tuple-element.13), channel_id=1, source_target_pairs={{0,1},{1,0},{2,3},{3,2},{4,5},{5,4},{6,7},{7,6},{8,9},{9,8},{10,11... | collective-permute-start | bytes 786440 | tf_op jit(solution)/shard_map/ppermute | solution.py:223
  111.0 45.8 %collective-permute-start.7 = (f32[4,2,32,1024]{3,2,1,0:T(8,128)S(1)}, f32[4,2,32,1024]{3,2,1,0:T(8,128)S(1)}, u32[]{:S(2)}, u32[]{:S(2)}) collective-permute-start(f32[4,2,32,1024]{3,2,1,0:T(8,128)S(1)} %select_add_fusion), channel_id=1, source_target_pairs={{0,4},{1,5},{2,6},{3,7},{4,8},{5,9},{6,10},{7,11},{8,12},{9,13},{1... | collective-permute-start | bytes 3145736 | tf_op jit(solution)/shard_map/ppermute | solution.py:223
  111.5 6.4 %collective-permute-start.9 = (f32[2,2,128,128]{3,2,1,0:T(8,128)S(1)}, f32[2,2,128,128]{3,2,1,0:T(8,128)S(1)}, u32[]{:S(2)}, u32[]{:S(2)}) collective-permute-start(f32[2,2,128,128]{3,2,1,0:T(8,128)S(1)} %add.46), channel_id=1, source_target_pairs={{0,2},{1,3},{2,0},{3,1},{4,6},{5,7},{6,4},{7,5},{8,10},{9,11},{10,... | collective-permute-start | bytes 786440 | tf_op jit(solution)/shard_map/ppermute | solution.py:223
  117.9 24.3 %collective-permute-start.10 = (f32[2,2,128,128]{3,2,1,0:T(8,128)S(1)}, f32[2,2,128,128]{3,2,1,0:T(8,128)S(1)}, u32[]{:S(2)}, u32[]{:S(2)}) collective-permute-start(f32[2,2,128,128]{3,2,1,0:T(8,128)S(1)} %add.47), channel_id=1, source_target_pairs={{0,4},{1,5},{2,6},{3,7},{4,0},{5,1},{6,2},{7,3},{8,12},{9,13},{10,... | collective-permute-start | bytes 786440 | tf_op jit(solution)/shard_map/ppermute | solution.py:223
  142.3 13.8 %collective-permute-start.11 = (f32[2,2,128,128]{3,2,1,0:T(8,128)S(1)}, f32[2,2,128,128]{3,2,1,0:T(8,128)S(1)}, u32[]{:S(2)}, u32[]{:S(2)}) collective-permute-start(f32[2,2,128,128]{3,2,1,0:T(8,128)S(1)} %add.48), channel_id=1, source_target_pairs={{0,8},{1,9},{2,10},{3,11},{4,12},{5,13},{6,14},{7,15},{8,0},{9,1},... | collective-permute-start | bytes 786440 | tf_op jit(solution)/shard_map/ppermute | solution.py:223

commit v2 on v1

--- a/solution.py
+++ b/solution.py
@@ -1,5 +1,4 @@
 import functools
-import math
 
 import jax
 import jax.numpy as jnp
@@ -219,8 +218,276 @@
     )(row_offset, col_offset, *pieces, probe_modes, amplitude, tables)
 
 
-def permute(value, pairs):
-    return lax.ppermute(value, "tile", pairs)
+def push(src, dst, send_sem, recv_sem, partner):
+    return pltpu.make_async_remote_copy(
+        src_ref=src,
+        dst_ref=dst,
+        send_sem=send_sem,
+        recv_sem=recv_sem,
+        device_id={"tile": partner},
+        device_id_type=pl.DeviceIdType.MESH,
+    )
+
+
+def greet(partners):
+    barrier = pltpu.get_barrier_semaphore()
+    for partner in partners:
+        pl.semaphore_signal(
+            barrier, inc=1, device_id={"tile": partner}, device_id_type=pl.DeviceIdType.MESH
+        )
+    pl.semaphore_wait(barrier, len(partners))
+
+
+def flipped(index, step):
+    bit = (index // step) % 2
+    return index + step * (1 - 2 * bit), bit
+
+
+def gather_kernel(tiles, own, first, second, third, fourth, z_out, z_in, y_out, y_in, a_out, a_in, b_out, b_in):
+    index = lax.axis_index("tile")
+    other_core, core = flipped(index, 2**0)
+    other_chip, odd = flipped(index, 2)
+    ahead, behind = (index + tiles - 4) % tiles, (index + 4) % tiles
+    planes = own.shape[0]
+    greet([other_core, other_chip, ahead, behind])
+
+    def far(k):
+        return push(own.at[k], fourth.at[k], z_out.at[k], z_in.at[k], ahead)
+
+    def across(source, k):
+        return push(source.at[k], second.at[k], y_out.at[k], y_in.at[k], other_chip)
+
+    def beside(source, k):
+        return push(source.at[k], first.at[k], a_out.at[k], a_in.at[k], other_core)
+
+    def beside_third(source, k):
+        return push(source.at[k], third.at[k], b_out.at[k], b_in.at[k], other_core)
+
+    for k in range(planes):
+        far(k).start()
+
+    @pl.when(odd == 1)
+    def _():
+        for k in range(planes):
+            across(own, k).start()
+
+    @pl.when(core == 1)
+    def _():
+        for k in range(planes):
+            beside(own, k).start()
+
+    for k in range(planes + 1):
+        if k < planes:
+            far(k).wait_recv()
+
+            @pl.when(odd == 0)
+            def _():
+                across(fourth, k).start()
+
+            @pl.when(core == 0)
+            def _():
+                beside_third(fourth, k).start()
+
+        if k > 0:
+            across(fourth, k - 1).wait_recv()
+
+            @pl.when(core == 0)
+            def _():
+                beside(second, k - 1).start()
+
+            @pl.when(core == 1)
+            def _():
+                beside_third(second, k - 1).start()
+
+    for k in range(planes):
+        beside(second, k).wait_recv()
+        beside_third(second, k).wait_recv()
+    for k in range(planes):
+        far(k).wait_send()
+        across(own, k).wait_send()
+        beside(own, k).wait_send()
+        beside_third(second, k).wait_send()
+
+
+def gather_pieces(slices):
+    slice_count, parts, rows_here, cols_here = slices.shape
+    planes = slice_count * parts
+    flat = slices.reshape(planes, rows_here, cols_here)
+    anywhere = pl.BlockSpec(memory_space=pl.ANY)
+    got = pl.pallas_call(
+        functools.partial(gather_kernel, lax.axis_size("tile")),
+        out_shape=[jax.ShapeDtypeStruct(flat.shape, jnp.float32)] * 4,
+        in_specs=[anywhere],
+        out_specs=[anywhere] * 4,
+        scratch_shapes=[pltpu.SemaphoreType.DMA((planes,))] * 8,
+        compiler_params=pltpu.CompilerParams(collective_id=0, has_side_effects=True),
+        name="gather_tiles",
+    )(flat)
+    return [slices] + [piece.reshape(slices.shape) for piece in got]
+
+
+def scatter_kernel(tiles, steps, share0, share1, share2, share3, share4, terms, out, terms_out, *refs):
+    acc0, acc2, acc4, from_a, from_b, from_chip, from_far, gathered, partial = refs[:9]
+    inboxes = refs[9 : 9 + steps]
+    load_sem, a_out, a_in, b_out, b_in, y_out, y_in, z_out, z_in, p_out, p_in = refs[9 + steps :]
+    index = lax.axis_index("tile")
+    other_core, core = flipped(index, 2**0)
+    other_chip, odd = flipped(index, 2)
+    ahead, behind = (index + tiles - 4) % tiles, (index + 4) % tiles
+    planes = share0.shape[0]
+    partners, bits = [], []
+    for b in range(steps):
+        partner, bit = flipped(index, 2**b)
+        partners.append(partner)
+        bits.append(bit)
+    greet([ahead, behind] + partners)
+
+    def beside(k):
+        return push(share1.at[k], from_a.at[k], a_out.at[k], a_in.at[k], other_core)
+
+    def beside_third(k):
+        return push(share3.at[k], from_b.at[k], b_out.at[k], b_in.at[k], other_core)
+
+    def across(k):
+        return push(acc2.at[k], from_chip.at[k], y_out.at[k], y_in.at[k], other_chip)
+
+    def far(k):
+        return push(acc4.at[k], from_far.at[k], z_out.at[k], z_in.at[k], behind)
+
+    local = ((share0, acc0), (share2, acc2), (share4, acc4))
+
+    def load(i, k):
+        return pltpu.make_async_copy(local[i][0].at[k], local[i][1].at[k], load_sem.at[i, k])
+
+    for k in range(planes):
+        beside(k).start()
+        beside_third(k).start()
+        for i in range(3):
+            load(i, k).start()
+
+    bases, sizes = [0], [terms.shape[0]]
+    for b in range(steps):
+        sizes.append(sizes[-1] // 2)
+        bases.append(bases[-1] + bits[b] * sizes[-1])
+
+    def region(b):
+        return pl.ds(pl.multiple_of(bases[b], SUBLANES), sizes[b])
+
+    def reduce_copy(b):
+        start = bases[b] + (1 - bits[b]) * sizes[b + 1]
+        away = pl.ds(pl.multiple_of(start, SUBLANES), sizes[b + 1])
+        return push(partial.at[away], inboxes[b], p_out.at[b], p_in.at[b], partners[b])
+
+    def spread_copy(b, base_index):
+        part = region(base_index) if base_index is not None else None
+        return push(
+            gathered.at[part], gathered.at[part], p_out.at[steps + b], p_in.at[steps + b], partners[b]
+        )
+
+    partial[...] = terms[...]
+
+    def probe_turn(turn):
+        if turn > 2 * steps:
+            return
+        if 0 < turn <= steps:
+            b = turn - 1
+            reduce_copy(b).wait_recv()
+            partial[region(b + 1)] += inboxes[b][...]
+            if turn == steps:
+                gathered[region(steps)] = partial[region(steps)]
+        elif turn > steps:
+            spread_copy(2 * steps - turn, 2 * steps - turn + 1).wait_recv()
+        if turn < steps:
+            reduce_copy(turn).start()
+        elif turn < 2 * steps:
+            b = 2 * steps - 1 - turn
+            spread_copy(b, b + 1).start()
+
+    for k in range(planes + 1):
+        probe_turn(k)
+        if k < planes:
+            for i in range(3):
+                load(i, k).wait()
+            beside(k).wait_recv()
+            beside_third(k).wait_recv()
+
+            @pl.when(core == 0)
+            def _():
+                acc2[k] += from_a[k]
+                acc4[k] += from_b[k]
+
+            @pl.when(core == 1)
+            def _():
+                acc2[k] += from_b[k]
+                acc0[k] += from_a[k]
+
+            across(k).start()
+
+            @pl.when(odd == 1)
+            def _():
+                far(k).start()
+
+        if k > 0:
+            across(k - 1).wait_recv()
+
+            @pl.when(odd == 0)
+            def _():
+                acc4[k - 1] += from_chip[k - 1]
+                far(k - 1).start()
+
+            @pl.when(odd == 1)
+            def _():
+                acc0[k - 1] += from_chip[k - 1]
+
+    for turn in range(planes + 1, 2 * steps + 1):
+        probe_turn(turn)
+    for k in range(planes):
+        far(k).wait_recv()
+        out[k] = acc0[k] + from_far[k]
+    terms_out[...] = gathered[...]
+    for k in range(planes):
+        beside(k).wait_send()
+        beside_third(k).wait_send()
+        across(k).wait_send()
+        far(k).wait_send()
+    for b in range(steps):
+        reduce_copy(b).wait_send()
+        spread_copy(b, b + 1).wait_send()
+
+
+def scatter_shares(shares, probe_terms):
+    slice_count, parts, rows_here, cols_here = shares[0].shape
+    planes = slice_count * parts
+    flat_shape = (planes, rows_here, cols_here)
+    flat = [share.reshape(flat_shape) for share in shares]
+    side = probe_terms.shape[-1]
+    terms = probe_terms.reshape(-1, side)
+    tiles = lax.axis_size("tile")
+    steps = tiles.bit_length() - 1
+    assert tiles == 2**steps and tiles > 8
+    anywhere = pl.BlockSpec(memory_space=pl.ANY)
+    vmem = pl.BlockSpec(memory_space=pltpu.VMEM)
+    dma = pltpu.SemaphoreType.DMA
+    out, summed = pl.pallas_call(
+        functools.partial(scatter_kernel, tiles, steps),
+        out_shape=[
+            jax.ShapeDtypeStruct(flat_shape, jnp.float32),
+            jax.ShapeDtypeStruct(terms.shape, jnp.float32),
+        ],
+        in_specs=[anywhere] * len(flat) + [vmem],
+        out_specs=[vmem, vmem],
+        scratch_shapes=[pltpu.VMEM(flat_shape, jnp.float32)] * 7
+        + [pltpu.VMEM(terms.shape, jnp.float32)] * 2
+        + [pltpu.VMEM((terms.shape[0] >> (b + 1), side), jnp.float32) for b in range(steps)]
+        + [dma((3, planes))]
+        + [dma((planes,))] * 8
+        + [dma((2 * steps,))] * 2,
+        compiler_params=pltpu.CompilerParams(
+            collective_id=1, has_side_effects=True, vmem_limit_bytes=32 << 20
+        ),
+        name="scatter_tiles",
+    )(*flat, terms)
+    return out.reshape(shares[0].shape), summed.reshape(probe_terms.shape)
 
 
 def on_device(slices, probe_modes, row_offset, col_offset, amplitude):
@@ -228,38 +495,9 @@
     rows_here = slices.shape[2]
     reach = (side - 2) // rows_here + 1
     assert reach == 4
-    tiles = lax.axis_size("tile")
-    index = lax.axis_index("tile")
-    core = index % 2
-    odd_chip = (index // 2) % 2
-    swap_core = [(s, s ^ 1) for s in range(tiles)]
-    swap_chip = [(s, s ^ 2) for s in range(tiles)]
-    ahead = [(s, (s - 4) % tiles) for s in range(tiles)]
-    behind = [(s, (s + 4) % tiles) for s in range(tiles)]
-
-    fourth = permute(slices, ahead)
-    second = permute(jnp.where(odd_chip == 1, slices, fourth), swap_chip)
-    first = permute(jnp.where(core == 1, slices, second), swap_core)
-    third = permute(jnp.where(core == 1, second, fourth), swap_core)
-    pieces = [slices, first, second, third, fourth]
-
+    pieces = gather_pieces(slices)
     *shares, probe_terms = run_windows(pieces, probe_modes, row_offset, col_offset, amplitude)
-
-    got_first = permute(shares[1], swap_core)
-    got_third = permute(shares[3], swap_core)
-    low_core = core == 0
-    sum_second = shares[2] + jnp.where(low_core, got_first, got_third)
-    got_second = permute(sum_second, swap_chip)
-    even = odd_chip == 0
-    sum_fourth = shares[4] + jnp.where(low_core, got_third, 0.0) + jnp.where(even, got_second, 0.0)
-    own = shares[0] + jnp.where(low_core, 0.0, got_first) + jnp.where(even, 0.0, got_second)
-    slice_grad = own + permute(sum_fourth, behind)
-
-    step = 1
-    while step < tiles:
-        probe_terms = probe_terms + permute(probe_terms, [(s, s ^ step) for s in range(tiles)])
-        step *= 2
-    return (slice_grad, probe_terms)
+    return scatter_shares(shares, probe_terms)
 
 
 def solution(mesh):

time: 159 us -> 99.3 us (0.62)
  waiting for transfers between devices: 117 us -> 0 us
  Pallas kernels: 15.6 us -> 96.1 us
  starting transfers between devices: 15.4 us -> 0 us
  other arithmetic: 7.76 us -> 0 us
    ppermute x12 -> x0, waiting for transfers between devices: 117 us -> none  [permute(): return lax.ppermute(value, 'tile', pairs)]
    pallas_call x0 -> x2, Pallas kernels: none -> 81 us  [the longest x1 48.7 us: scatter_shares(): pl.pallas_call(functools.partial(scatter_kernel, tiles, steps), out_shape...]
    ppermute x12 -> x0, starting transfers between devices: 15.4 us -> none  [permute(): return lax.ppermute(value, 'tile', pairs)]
    add x7 -> x0, other arithmetic: 6.26 us -> none  [the longest x1 2.47 us: on_device(): sum_second = shares[2] + jnp.where(low_core, got_first, got_third)]
  transfers between devices with their start and end apart: 12 -> 0, of which waited for: 10 -> 0; matrix products, arithmetic and copies ran while one was open for 2% -> 0% of each run, Pallas kernels for 0% -> 0%
where the time goes in v2:
time: 99.3 us; the launch traced here: 99.1 us
  Pallas kernels  96.1 us (97%)
  local copies, waits for them, and re-layouts  2.32 us (2%)
    pallas_call x1, Pallas kernels, scatter_shares(): pl.pallas_call(functools.partial(scatter_kernel, tiles, steps), out_shape...  48.7 us
    pallas_call x1, Pallas kernels, gather_pieces(): pl.pallas_call(functools.partial(gather_kernel, lax.axis_size('tile')), o...  32.4 us
    pallas_call x1, Pallas kernels, run_windows(): pl.pallas_call(functools.partial(window_kernel, count), out_shape=[jax.Sh...  15.1 us
    unnamed x10, local copies, waits for them, and re-layouts  2.32 us

profile of v2, /device:TPU:0, one launch (start us, length us, event | category | flops | bytes accessed | tf_op | source)
XLA Modules:
  0.0 99.1 jit_solution(2258690262116972614)
XLA Ops:
  0.6 0.0 copy-start
  0.6 0.0 copy-start.1
  0.6 32.4 %gather_tiles.1 = (f32[8,32,1024]{2,1,0:T(8,128)}, f32[8,32,1024]{2,1,0:T(8,128)}, f32[8,32,1024]{2,1,0:T(8,128)}, f32[8,32,1024]{2,1,0:T(8,128)}) custom-call(f32[8,32,1024]{2,1,0:T(8,128)} %bitcast.21), custom_call_target="tpu_custom_call" | custom-call | tf_op jit(solution)/shard_map/gather_tiles/pallas_call | solution.py:317
  33.0 0.0 copy-start.2
  33.0 0.0 copy-start.3
  33.0 0.0 copy-done
  33.0 0.0 copy-done.1
  33.1 0.6 copy-done.2
  33.7 0.0 copy-done.3
  33.7 15.1 %windows.1 = (f32[4,2,32,1024]{3,2,1,0:T(8,128)S(1)}, f32[4,2,32,1024]{3,2,1,0:T(8,128)S(1)}, f32[4,2,32,1024]{3,2,1,0:T(8,128)S(1)}, f32[4,2,32,1024]{3,2,1,0:T...) custom-call(s32[4]{0:T(128)S(1)} %copy-done.2, s32[4]{0:T(128)S(1)} %copy-done.3, ...), custom_call_target="tpu_custom_call" | custom-call | tf_op jit(solution)/shard_map/windows/pallas_call | solution.py:202
  48.8 48.7 %scatter_tiles.1 = (f32[8,32,1024]{2,1,0:T(8,128)S(1)}, f32[512,128]{1,0:T(8,128)S(1)}) custom-call(f32[8,32,1024]{2,1,0:T(8,128)S(1)} %bitcast.14, f32[8,32,1024]{2,1,0:T(8,128)S(1)} %bitcast.15, f32[8,32,1024]{2,1,0:T(8,128)S(1)} %bitcast.16, f32[8,32,1024]{2,1,0:T(8,128)S(1)} %bitcast.17, f32[8,32,1024]{2,1,0:T(8,128)S(1)} %bitcast.18, ...), custom_call_target="tpu_custom_call" | custom-call | tf_op jit(solution)/shard_map/scatter_tiles/pallas_call | solution.py:471
  97.4 1.0 copy.10
  98.4 0.7 copy.11
Async XLA Ops:
  0.6 32.4 %copy-start = (f32[2,2,128,128]{3,2,1,0:T(8,128)S(1)}, f32[2,2,128,128]{3,2,1,0:T(8,128)}, u32[]{:S(2)}) copy-start(f32[2,2,128,128]{3,2,1,0:T(8,128)} %refs_5_.1) | copy-start | bytes 786436
  0.6 32.4 %copy-start.1 = (f32[4,128,128]{2,1,0:T(8,128)S(1)}, f32[4,128,128]{2,1,0:T(8,128)}, u32[]{:S(2)}) copy-start(f32[4,128,128]{2,1,0:T(8,128)} %refs_6_.1) | copy-start | bytes 786436
  33.0 0.7 copy-start.2
  33.0 0.7 copy-start.3

commit v3 on v2

--- a/solution.py
+++ b/solution.py
@@ -359,12 +359,6 @@
     def load(i, k):
         return pltpu.make_async_copy(local[i][0].at[k], local[i][1].at[k], load_sem.at[i, k])
 
-    for k in range(planes):
-        beside(k).start()
-        beside_third(k).start()
-        for i in range(3):
-            load(i, k).start()
-
     bases, sizes = [0], [terms.shape[0]]
     for b in range(steps):
         sizes.append(sizes[-1] // 2)
@@ -403,45 +397,60 @@
             b = 2 * steps - 1 - turn
             spread_copy(b, b + 1).start()
 
-    for k in range(planes + 1):
-        probe_turn(k)
-        if k < planes:
-            for i in range(3):
-                load(i, k).wait()
-            beside(k).wait_recv()
-            beside_third(k).wait_recv()
-
-            @pl.when(core == 0)
-            def _():
-                acc2[k] += from_a[k]
-                acc4[k] += from_b[k]
-
-            @pl.when(core == 1)
-            def _():
-                acc2[k] += from_b[k]
-                acc0[k] += from_a[k]
-
-            across(k).start()
+    probe_turn(0)
+    for k in range(planes):
+        beside(k).start()
+        beside_third(k).start()
+        for i in range(3):
+            load(i, k).start()
+
+    probe_turn(1)
+    for k in range(planes):
+        for i in range(3):
+            load(i, k).wait()
+        beside(k).wait_recv()
+        beside_third(k).wait_recv()
+
+        @pl.when(core == 0)
+        def _():
+            acc2[k] += from_a[k]
+            acc4[k] += from_b[k]
+
+        @pl.when(core == 1)
+        def _():
+            acc2[k] += from_b[k]
+            acc0[k] += from_a[k]
+
+        across(k).start()
+
+    turn_before = {0: 2, 1: 3, 3: 4, 4: 5, 5: 6}
+    for k in range(planes):
+        if k in turn_before:
+            probe_turn(turn_before[k])
+        if k == 0:
 
             @pl.when(odd == 1)
             def _():
-                far(k).start()
-
-        if k > 0:
-            across(k - 1).wait_recv()
-
-            @pl.when(odd == 0)
-            def _():
-                acc4[k - 1] += from_chip[k - 1]
-                far(k - 1).start()
-
-            @pl.when(odd == 1)
-            def _():
-                acc0[k - 1] += from_chip[k - 1]
-
-    for turn in range(planes + 1, 2 * steps + 1):
+                far(0).start()
+
+        across(k).wait_recv()
+
+        @pl.when(odd == 0)
+        def _():
+            acc4[k] += from_chip[k]
+            far(k).start()
+
+        @pl.when(odd == 1)
+        def _():
+            acc0[k] += from_chip[k]
+            if k + 1 < planes:
+                far(k + 1).start()
+
+    for turn in range(7, 2 * steps):
         probe_turn(turn)
     for k in range(planes):
+        if k == planes - 1:
+            probe_turn(2 * steps)
         far(k).wait_recv()
         out[k] = acc0[k] + from_far[k]
     terms_out[...] = gathered[...]

time: 99.3 us -> 98 us (0.987)
  Pallas kernels: 96.1 us -> 94 us
    pallas_call x1, Pallas kernels: 48.7 us -> 46.6 us  [scatter_shares(): pl.pallas_call(functools.partial(scatter_kernel, tiles, steps), out_shape...]
where the time goes in v3:
time: 98 us; the launch traced here: 97 us
  Pallas kernels  94 us (96%)
  local copies, waits for them, and re-layouts  2.32 us (2%)
    pallas_call x1, Pallas kernels, scatter_shares(): pl.pallas_call(functools.partial(scatter_kernel, tiles, steps), out_shape...  46.6 us
    pallas_call x1, Pallas kernels, gather_pieces(): pl.pallas_call(functools.partial(gather_kernel, lax.axis_size('tile')), o...  32.4 us
    pallas_call x1, Pallas kernels, run_windows(): pl.pallas_call(functools.partial(window_kernel, count), out_shape=[jax.Sh...  15.1 us
    unnamed x10, local copies, waits for them, and re-layouts  2.32 us

profile of v3, /device:TPU:0, one launch (start us, length us, event | category | flops | bytes accessed | tf_op | source)
XLA Modules:
  0.0 97.0 jit_solution(3314495650191611581)
XLA Ops:
  0.6 0.0 copy-start
  0.6 0.0 copy-start.1
  0.6 32.4 %gather_tiles.1 = (f32[8,32,1024]{2,1,0:T(8,128)}, f32[8,32,1024]{2,1,0:T(8,128)}, f32[8,32,1024]{2,1,0:T(8,128)}, f32[8,32,1024]{2,1,0:T(8,128)}) custom-call(f32[8,32,1024]{2,1,0:T(8,128)} %bitcast.21), custom_call_target="tpu_custom_call" | custom-call | tf_op jit(solution)/shard_map/gather_tiles/pallas_call | solution.py:317
  33.0 0.0 copy-start.2
  33.0 0.0 copy-start.3
  33.0 0.0 copy-done
  33.0 0.0 copy-done.1
  33.1 0.6 copy-done.2
  33.7 0.0 copy-done.3
  33.7 15.1 %windows.1 = (f32[4,2,32,1024]{3,2,1,0:T(8,128)S(1)}, f32[4,2,32,1024]{3,2,1,0:T(8,128)S(1)}, f32[4,2,32,1024]{3,2,1,0:T(8,128)S(1)}, f32[4,2,32,1024]{3,2,1,0:T...) custom-call(s32[4]{0:T(128)S(1)} %copy-done.2, s32[4]{0:T(128)S(1)} %copy-done.3, ...), custom_call_target="tpu_custom_call" | custom-call | tf_op jit(solution)/shard_map/windows/pallas_call | solution.py:202
  48.8 46.6 %scatter_tiles.1 = (f32[8,32,1024]{2,1,0:T(8,128)S(1)}, f32[512,128]{1,0:T(8,128)S(1)}) custom-call(f32[8,32,1024]{2,1,0:T(8,128)S(1)} %bitcast.14, f32[8,32,1024]{2,1,0:T(8,128)S(1)} %bitcast.15, f32[8,32,1024]{2,1,0:T(8,128)S(1)} %bitcast.16, f32[8,32,1024]{2,1,0:T(8,128)S(1)} %bitcast.17, f32[8,32,1024]{2,1,0:T(8,128)S(1)} %bitcast.18, ...), custom_call_target="tpu_custom_call" | custom-call | tf_op jit(solution)/shard_map/scatter_tiles/pallas_call | solution.py:480
  95.3 1.0 %copy.10 = f32[4,2,32,1024]{3,2,1,0:T(8,128)} copy(f32[4,2,32,1024]{3,2,1,0:T(8,128)S(1)} %bitcast.13) | data formatting | bytes 2097152
  96.3 0.7 copy.11
Async XLA Ops:
  0.6 32.4 %copy-start = (f32[2,2,128,128]{3,2,1,0:T(8,128)S(1)}, f32[2,2,128,128]{3,2,1,0:T(8,128)}, u32[]{:S(2)}) copy-start(f32[2,2,128,128]{3,2,1,0:T(8,128)} %refs_5_.1) | copy-start | bytes 786436
  0.6 32.4 %copy-start.1 = (f32[4,128,128]{2,1,0:T(8,128)S(1)}, f32[4,128,128]{2,1,0:T(8,128)}, u32[]{:S(2)}) copy-start(f32[4,128,128]{2,1,0:T(8,128)} %refs_6_.1) | copy-start | bytes 786436
  33.0 0.7 copy-start.2
  33.0 0.7 copy-start.3

commit v4 on v3

--- a/solution.py
+++ b/solution.py
@@ -12,6 +12,7 @@
 FRESNEL = 0.75
 LANES = 128
 SUBLANES = 8
+CUTS = 2
 
 
 def field_tables(side):
@@ -311,8 +312,8 @@
 
 def gather_pieces(slices):
     slice_count, parts, rows_here, cols_here = slices.shape
-    planes = slice_count * parts
-    flat = slices.reshape(planes, rows_here, cols_here)
+    planes = slice_count * parts * CUTS
+    flat = slices.reshape(planes, rows_here // CUTS, cols_here)
     anywhere = pl.BlockSpec(memory_space=pl.ANY)
     got = pl.pallas_call(
         functools.partial(gather_kernel, lax.axis_size("tile")),
@@ -423,7 +424,7 @@
 
         across(k).start()
 
-    turn_before = {0: 2, 1: 3, 3: 4, 4: 5, 5: 6}
+    turn_before = {0: 2, 2: 3, 5: 4, 7: 5, 9: 6}
     for k in range(planes):
         if k in turn_before:
             probe_turn(turn_before[k])
@@ -466,8 +467,8 @@
 
 def scatter_shares(shares, probe_terms):
     slice_count, parts, rows_here, cols_here = shares[0].shape
-    planes = slice_count * parts
-    flat_shape = (planes, rows_here, cols_here)
+    planes = slice_count * parts * CUTS
+    flat_shape = (planes, rows_here // CUTS, cols_here)
     flat = [share.reshape(flat_shape) for share in shares]
     side = probe_terms.shape[-1]
     terms = probe_terms.reshape(-1, side)

time: 98 us -> 98.3 us (level)
  Pallas kernels: 94 us -> 95.1 us
    pallas_call x1, Pallas kernels: 46.6 us -> 47.8 us  [scatter_shares(): pl.pallas_call(functools.partial(scatter_kernel, tiles, steps), out_shape...]
where the time goes in v4:
time: 98.3 us; the launch traced here: 98.1 us
  Pallas kernels  95.1 us (97%)
  local copies, waits for them, and re-layouts  2.32 us (2%)
    pallas_call x1, Pallas kernels, scatter_shares(): pl.pallas_call(functools.partial(scatter_kernel, tiles, steps), out_shape...  47.8 us
    pallas_call x1, Pallas kernels, gather_pieces(): pl.pallas_call(functools.partial(gather_kernel, lax.axis_size('tile')), o...  32.3 us
    pallas_call x1, Pallas kernels, run_windows(): pl.pallas_call(functools.partial(window_kernel, count), out_shape=[jax.Sh...  15.1 us
    unnamed x10, local copies, waits for them, and re-layouts  2.32 us

profile of v4, /device:TPU:0, one launch (start us, length us, event | category | flops | bytes accessed | tf_op | source)
XLA Modules:
  0.0 98.1 jit_solution(5071362301768926884)
XLA Ops:
  0.6 0.0 copy-start
  0.6 0.0 copy-start.1
  0.6 32.3 %gather_tiles.1 = (f32[16,16,1024]{2,1,0:T(8,128)}, f32[16,16,1024]{2,1,0:T(8,128)}, f32[16,16,1024]{2,1,0:T(8,128)}, f32[16,16,1024]{2,1,0:T(8,128)}) custom-call(f32[16,16,1024]{2,1,0:T(8,128)} %bitcast.21), custom_call_target="tpu_custom_call" | custom-call | tf_op jit(solution)/shard_map/gather_tiles/pallas_call | solution.py:318
  32.9 0.0 copy-start.2
  33.0 0.0 copy-start.3
  33.0 0.0 copy-done
  33.0 0.0 copy-done.1
  33.0 0.6 copy-done.2
  33.6 0.0 copy-done.3
  33.6 15.1 %windows.1 = (f32[4,2,32,1024]{3,2,1,0:T(8,128)S(1)}, f32[4,2,32,1024]{3,2,1,0:T(8,128)S(1)}, f32[4,2,32,1024]{3,2,1,0:T(8,128)S(1)}, f32[4,2,32,1024]{3,2,1,0:T...) custom-call(s32[4]{0:T(128)S(1)} %copy-done.2, s32[4]{0:T(128)S(1)} %copy-done.3, ...), custom_call_target="tpu_custom_call" | custom-call | tf_op jit(solution)/shard_map/windows/pallas_call | solution.py:203
  48.7 47.8 %scatter_tiles.1 = (f32[16,16,1024]{2,1,0:T(8,128)S(1)}, f32[512,128]{1,0:T(8,128)S(1)}) custom-call(f32[16,16,1024]{2,1,0:T(8,128)S(1)} %bitcast.14, f32[16,16,1024]{2,1,0:T(8,128)S(1)} %bitcast.15, f32[16,16,1024]{2,1,0:T(8,128)S(1)} %bitcast.16, f32[16,16,1024]{2,1,0:T(8,128)S(1)} %bitcast.17, f32[16,16,1024]{2,1,0:T(8,128)S(1)} %bitcast.18, ...), custom_call_target="tpu_custom_call" | custom-call | tf_op jit(solution)/shard_map/scatter_tiles/pallas_call | solution.py:481
  96.5 1.0 copy.10
  97.4 0.7 copy.11
Async XLA Ops:
  0.6 32.3 %copy-start = (f32[2,2,128,128]{3,2,1,0:T(8,128)S(1)}, f32[2,2,128,128]{3,2,1,0:T(8,128)}, u32[]{:S(2)}) copy-start(f32[2,2,128,128]{3,2,1,0:T(8,128)} %refs_5_.1) | copy-start | bytes 786436
  0.6 32.3 %copy-start.1 = (f32[4,128,128]{2,1,0:T(8,128)S(1)}, f32[4,128,128]{2,1,0:T(8,128)}, u32[]{:S(2)}) copy-start(f32[4,128,128]{2,1,0:T(8,128)} %refs_6_.1) | copy-start | bytes 786436
  32.9 0.7 copy-start.2
  33.0 0.7 copy-start.3
